TPU v7x, 256 devices: a whole 4x4x8 slice. The times are simulated.
256 devices in a mesh: gx: 32 (over y, x, core), gy: 8 (over z).
Axes of the slice: x: 4, y: 4, z: 8, core: 2. Of those that a mesh axis runs over, the one named last changes fastest.
Arguments:
- displacement: float32 [3, 32, 256, 1024], P(None, None, 'gx', 'gy'), may hold values from -6 to 6
- velocity: float32 [3, 32, 256, 1024], P(None, None, 'gx', 'gy'), may hold values from -6 to 6
- slopes: float32 [2, 32, 256, 1024], P(None, None, 'gx', 'gy'), may hold values from -0.5 to 0.5
- stretch: float32 [32, 256, 1024], P(None, 'gx', 'gy'), may hold values from 0.6 to 1.4
- moduli: float32 [2, 32, 256, 1024], P(None, None, 'gx', 'gy'), may hold values from 0.3 to 1
- buoyancy: float32 [32, 256, 1024], P(None, 'gx', 'gy'), may hold values from 0.5 to 1.5
- probes: float32 [4, 512, 128], P(None, 'gy'), may hold values from -0.0017089844 to 0.0017089844
Outputs:
- final_displacement: float32 [3, 32, 256, 1024], P(None, None, 'gx', 'gy')
- basis: float32 [128, 48, 128], P('gx', 'gy')
- factor: float32 [128, 128], replicated
All inputs are finite; a program needn't handle non-finite values.
Results may differ from a plain program's by a relative error of at most 0.0003.
Values sent between devices are 32-bit elements; how exact they have to be, the bound alone decides.
A program may use at most 64 MiB of HBM per device.

v0:
```python
import math
import jax
import jax.numpy as jnp
from jax import lax
from jax.sharding import PartitionSpec as P

STEPS = 4
time_step = 0.12


def extended(block, sides, width):
    for axis, dim in sides:
        count = lax.axis_size(axis)
        forward = [(i, i + 1) for i in range(count - 1)]
        backward = [(target, source) for source, target in forward]
        low = lax.ppermute(
            lax.slice_in_dim(block, block.shape[dim] - width, None, axis=dim), axis, forward
        )
        high = lax.ppermute(lax.slice_in_dim(block, 0, width, axis=dim), axis, backward)
        block = jnp.concatenate([low, block, high], axis=dim)
    return block


def fourth(values, dimension):
    length_out = values.shape[dimension] - 4

    def segment(offset):
        return lax.slice_in_dim(values, offset, offset + length_out, axis=dimension)

    return (segment(0) - segment(4) + 8.0 * (segment(3) - segment(1))) / 12.0


def vertical(values):
    padded = jnp.pad(values, ((0, 0), (2, 2), (0, 0), (0, 0)))
    return fourth(padded, 1)


def gradient(padded, slope_x, slope_y, stretch):
    d_x = fourth(padded[:, :, :, 2:-2], 2)
    d_y = fourth(padded[:, :, 2:-2, :], 3)
    d_r = vertical(padded[:, :, 2:-2, 2:-2])
    return jnp.stack([d_x + slope_x * d_r, d_y + slope_y * d_r, stretch * d_r], axis=1)


def stresses(gradients, lame, shear):
    divergence = gradients[0, 0] + gradients[1, 1] + gradients[2, 2]
    pressure = lame * divergence
    return jnp.stack(
        [
            pressure + 2.0 * shear * gradients[0, 0],
            pressure + 2.0 * shear * gradients[1, 1],
            pressure + 2.0 * shear * gradients[2, 2],
            shear * (gradients[0, 1] + gradients[1, 0]),
            shear * (gradients[0, 2] + gradients[2, 0]),
            shear * (gradients[1, 2] + gradients[2, 1]),
        ]
    )


def forces(padded, slope_x, slope_y, stretch):
    d_x = fourth(padded[:, :, :, 2:-2], 2)
    d_y = fourth(padded[:, :, 2:-2, :], 3)
    d_r = vertical(padded[:, :, 2:-2, 2:-2])
    rows_x = (0, 3, 4)
    rows_y = (3, 1, 5)
    rows_z = (4, 5, 2)
    return jnp.stack(
        [
            d_x[rows_x[component]]
            + slope_x * d_r[rows_x[component]]
            + d_y[rows_y[component]]
            + slope_y * d_r[rows_y[component]]
            + stretch * d_r[rows_z[component]]
            for component in range(3)
        ]
    )


def lower_factor(gram):
    order = gram.shape[0]
    positions = jnp.arange(order, dtype=jnp.int32)

    def column_step(column_index, lower):
        picker = (positions == column_index).astype(jnp.float32)
        column = jnp.dot(gram, picker, precision=lax.Precision.HIGHEST)
        row_of = jnp.dot(picker, lower, precision=lax.Precision.HIGHEST)
        column = column - jnp.dot(lower, row_of, precision=lax.Precision.HIGHEST)
        pivot = jnp.sqrt(jnp.sum(column * picker))
        entries = jnp.where(
            positions > column_index,
            column / pivot,
            jnp.where(positions == column_index, pivot, 0.0),
        )
        return lower + entries[:, None] * picker[None, :]

    return lax.fori_loop(0, order, column_step, jnp.zeros_like(gram))


def lower_inverse(lower):
    order = lower.shape[0]
    positions = jnp.arange(order, dtype=jnp.int32)

    def row_step(row_index, inverse):
        picker = (positions == row_index).astype(jnp.float32)
        row_of = jnp.dot(picker, lower, precision=lax.Precision.HIGHEST)
        pivot = jnp.sum(row_of * picker)
        fresh = (picker - jnp.dot(row_of, inverse, precision=lax.Precision.HIGHEST)) / pivot
        return inverse + picker[:, None] * fresh[None, :]

    return lax.fori_loop(0, order, row_step, jnp.zeros_like(lower))


def orthogonalize(tall_block, gram):
    lower = lower_factor(gram)
    inverse = lower_inverse(lower)
    result = jnp.dot(
        tall_block, inverse.T, precision=lax.Precision.HIGHEST, preferred_element_type=jnp.float32
    )
    return (result, lower.T)


def shards(displacement, velocity, slopes, stretch, moduli, buoyancy, probes):
    previous = displacement - time_step * velocity
    current = displacement
    for moment in range(STEPS):
        padded = extended(current, (("gx", 2), ("gy", 3)), 2)
        gradients = gradient(padded, slopes[0], slopes[1], stretch)
        stress = extended(stresses(gradients, moduli[0], moduli[1]), (("gx", 2), ("gy", 3)), 2)
        pushes = buoyancy * forces(stress, slopes[0], slopes[1], stretch)
        following = 2.0 * current - previous + time_step**2 * pushes
        velocities = (following - previous) / (2.0 * time_step)
        sampled = velocities[:, ::2, ::2, ::2]
        half_x = sampled.shape[2]
        rearranged = jnp.transpose(sampled, (2, 0, 1, 3)).reshape(-1, sampled.shape[3])
        sketch_term = jnp.dot(
            rearranged,
            probes[moment],
            precision=lax.Precision.HIGHEST,
            preferred_element_type=jnp.float32,
        ).reshape(half_x, -1, probes.shape[2])
        reduced = lax.psum_scatter(sketch_term, "gy", scatter_dimension=1, tiled=True)
        sketch = reduced if moment == 0 else sketch + reduced
        previous, current = (current, following)
    tall_block = sketch.reshape(-1, sketch.shape[2])
    rows_total = tall_block.shape[0] * lax.axis_size("gx") * lax.axis_size("gy")
    gram_local = jnp.dot(
        tall_block.T,
        tall_block,
        precision=lax.Precision.HIGHEST,
        preferred_element_type=jnp.float32,
    )
    gram_whole = lax.psum(gram_local, ("gx", "gy"))
    orthonormal, factor = orthogonalize(tall_block, gram_whole)
    basis = (math.sqrt(rows_total) * orthonormal).reshape(sketch.shape)
    return (current, basis, factor)


def solution(mesh):
    in_specs = (
        P(None, None, "gx", "gy"),
        P(None, None, "gx", "gy"),
        P(None, None, "gx", "gy"),
        P(None, "gx", "gy"),
        P(None, None, "gx", "gy"),
        P(None, "gx", "gy"),
        P(None, "gy", None),
    )
    out_specs = (P(None, None, "gx", "gy"), P("gx", "gy", None), P())
    return jax.shard_map(shards, mesh=mesh, in_specs=in_specs, out_specs=out_specs, check_vma=False)
```

profile of v0, /device:TPU:1, one launch (start us, length us, event | category | flops | bytes accessed | tf_op | source)
XLA Modules:
  0.0 1194.3 jit_solution(5939340690643367252)
XLA Ops:
  8.8 4.6 collective-permute-start
  18.1 4.4 collective-permute-done.1
  26.6 4.9 collective-permute-start.2
  35.1 3.8 fusion.119
  49.6 4.4 collective-permute-done.5
  59.1 3.6 collective-permute-start.6
  64.0 2.7 fusion.51
  71.9 3.0 fusion.94
  76.9 3.5 collective-permute-start.8
  82.4 4.0 collective-permute-done.9
  89.0 3.7 collective-permute-start.10
  101.8 3.0 collective-permute-start.12
  107.4 4.4 collective-permute-done.13
  117.2 5.1 collective-permute-start.14
  131.9 3.4 fusion.88
  136.6 2.9 collective-permute-start.16
  141.4 6.0 slice.1072
  150.9 3.6 collective-permute-start.18
  163.3 5.1 collective-permute-start.20
  171.9 6.0 slice.1074
  185.3 3.9 collective-permute-start.22
  198.7 3.0 fusion.82
  202.2 5.1 collective-permute-start.24
  225.0 5.1 collective-permute-start.28
  233.0 4.0 collective-permute-done.29
  243.1 3.7 collective-permute-start.30
  249.5 2.8 collective-permute-done.31
  257.1 3.4 fusion.76
  266.5 78.0 %all-reduce.14.cloned.1.call-done = f32[4,48,128]{2,0,1:T(4,128)} async-done(((f32[4,48,128]{2,0,1:T(4,128)}), f32[4,48,128]{2,0,1:T(4,128)}) %all-reduce.14.cloned.1.call-update) | async-done | bytes 98320
  347.2 245.3 %all-reduce.12.cloned.1.call-done = f32[128,128]{1,0:T(8,128)} async-done(((f32[128,128]{1,0:T(8,128)}), f32[128,128]{1,0:T(8,128)}) %all-reduce.12.cloned.1.call-update) | async-done | bytes 65552 | tf_op jit(solution)/shard_map/psum | solution.py:152
  592.5 363.3 %while.30 = (s32[]{:T(128)}, f32[128,128]{1,0:T(8,128)S(1)}, f32[128,128]{1,0:T(8,128)}, s32[]{:T(128)}, s32[]{:T(128)}) while((s32[]{:T(128)}, f32[128,128]{1,0:T(8,128)S(1)}, f32[128,128]{1,0:T(8,128)}, s32[]{:T(128)}, s32[]{:T(128)}) %tuple.125), condition=%wide.region_7.8_spmd.clone.clone, body=%wide.region_5.7_spmd.clone.clone.sunk | while | flops 673410 | bytes 332917 | solution.py:96
  956.5 230.0 %while.29 = (s32[]{:T(128)}, f32[128,128]{1,0:T(8,128)S(1)}, f32[128,128]{1,0:T(8,128)S(1)}, s32[]{:T(128)}, s32[]{:T(128)}) while((s32[]{:T(128)}, f32[128,128]{1,0:T(8,128)S(1)}, f32[128,128]{1,0:T(8,128)S(1)}, s32[]{:T(128)}, s32[]{:T(128)}) %tuple.128), condition=%wide.region_10.11_spmd.clone, body=%wide.region_8.10_spmd.clone.sunk | while | flops 460034 | bytes 265316 | solution.py:110
  (1541 shorter events, 643.5 us)
Async XLA Ops:
  7.2 337.4 %all-reduce.14.cloned.1.call-start = ((), (), s32[]{:S(2)}) async-start(), calls=%async_computation.1 | async-start | bytes 196608
  8.8 9.3 collective-permute-start
  13.4 9.1 collective-permute-start.1
  25.3 16.2 %collective-permute-start.3 = (f32[3,32,12,2]{1,3,2,0:T(2,128)}, f32[3,32,12,2]{1,3,2,0:T(2,128)}, u32[]{:S(2)}, u32[]{:S(2)}) collective-permute-start(f32[3,32,12,2]{1,3,2,0:T(2,128)} %get-tuple-element.276), channel_id=1, source_target_pairs={{1,0},{2,1},{3,2},{4,3},{5,4},{6,5},{7,6},{9,8},{10,9},{11,10},{12... | collective-permute-start | bytes 27656 | tf_op jit(solution)/shard_map/ppermute | solution.py:19
  26.6 13.8 %collective-permute-start.2 = (f32[3,32,12,2]{1,3,2,0:T(2,128)}, f32[3,32,12,2]{1,3,2,0:T(2,128)}, u32[]{:S(2)}, u32[]{:S(2)}) collective-permute-start(f32[3,32,12,2]{1,3,2,0:T(2,128)} %get-tuple-element.277), channel_id=1, source_target_pairs={{0,1},{1,2},{2,3},{3,4},{4,5},{5,6},{6,7},{8,9},{9,10},{10,11},{11... | collective-permute-start | bytes 27656 | tf_op jit(solution)/shard_map/ppermute | solution.py:16
  47.0 7.0 collective-permute-start.5
  59.1 10.4 collective-permute-start.6
  62.7 5.4 collective-permute-start.7
  76.9 5.5 collective-permute-start.8
  80.4 5.9 collective-permute-start.9
  89.0 9.1 collective-permute-start.10
  92.8 5.1 collective-permute-start.11
  101.8 5.6 collective-permute-start.12
  104.8 7.0 collective-permute-start.13
  117.2 13.2 %collective-permute-start.14 = (f32[6,32,12,2]{1,3,2,0:T(2,128)S(1)}, f32[6,32,12,2]{1,3,2,0:T(2,128)S(1)}, u32[]{:S(2)}, u32[]{:S(2)}) collective-permute-start(f32[6,32,12,2]{1,3,2,0:T(2,128)S(1)} %copy.329), channel_id=1, source_target_pairs={{0,1},{1,2},{2,3},{3,4},{4,5},{5,6},{6,7},{8,9},{9,10},{10,11},{11... | collective-permute-start | bytes 55304 | tf_op jit(solution)/shard_map/ppermute | solution.py:16
  122.3 5.7 collective-permute-start.15
  136.6 11.5 collective-permute-start.16
  139.5 8.6 collective-permute-start.17
  150.9 8.8 collective-permute-start.18
  154.5 4.8 collective-permute-start.19
  163.3 15.3 %collective-permute-start.20 = (f32[6,32,2,128]{3,1,2,0:T(8,128)S(1)}, f32[6,32,2,128]{3,1,2,0:T(8,128)S(1)}, u32[]{:S(2)}, u32[]{:S(2)}) collective-permute-start(f32[6,32,2,128]{3,1,2,0:T(8,128)S(1)} %get-tuple-element.294), channel_id=1, source_target_pairs={{0,8},{8,16},{16,24},{24,32},{32,40},{40,48},{48,56},{56,64},{64,7... | collective-permute-start | bytes 589832 | tf_op jit(solution)/shard_map/ppermute | solution.py:16
  168.4 10.2 collective-permute-start.21
  185.3 11.0 collective-permute-start.22
  189.3 5.7 collective-permute-start.23
  202.2 11.8 collective-permute-start.24
  207.3 6.7 collective-permute-start.25
  214.9 7.5 collective-permute-start.26
  225.0 8.0 collective-permute-start.28
  230.1 7.0 collective-permute-start.29
  243.1 11.6 collective-permute-start.30
  246.9 5.4 collective-permute-start.31
  265.2 327.3 %all-reduce.12.cloned.1.call-start = ((), (), s32[]{:S(2)}) async-start(), calls=%async_computation | async-start | bytes 131072 | tf_op jit(solution)/shard_map/psum | solution.py:152
  (44 other events, 211.1 us)
Sparse Core Ops, SparseCore 0:
  265.3 79.1 all-reduce.13
  351.5 240.9 all-reduce.11
where the time goes:
time: 1210 us; the launch traced here: 1190 us
  matrix products  475 us (39%)
  waiting for transfers between devices  362 us (30%)
  loops' own time  98.3 us (8%)
  starting transfers between devices  89 us (7%)
  local copies, waits for them, and re-layouts  85.4 us (7%)
  other arithmetic  68.3 us (6%)
  between operations  15.9 us (1%)
    psum x1, waiting for transfers between devices, shards(): gram_whole = lax.psum(gram_local, ('gx', 'gy'))  245 us
    dot_general x128, matrix products, column_step(): column = jnp.dot(gram, picker, precision=lax.Precision.HIGHEST)  124 us
    dot_general x128, matrix products, column_step(): column = column - jnp.dot(lower, row_of, precision=lax.Precision.HIGHEST)  108 us
    dot_general x128, matrix products, row_step(): jnp.dot(row_of, inverse, precision=lax.Precision.HIGHEST)  107 us
    dot_general x128, matrix products, row_step(): row_of = jnp.dot(picker, lower, precision=lax.Precision.HIGHEST)  105 us
    another operation x1, loops' own time, lower_factor(): return lax.fori_loop(0, order, column_step, jnp.zeros_like(gram))  94 us
    unnamed x3, waiting for transfers between devices  78.1 us
    ppermute x16, starting transfers between devices, extended(): lax.ppermute(lax.slice_in_dim(block, block.shape[dim] - width, None, axis...  62.5 us
  transfers between devices with their start and end apart: 34, of which 17 were waited for; matrix products, arithmetic and copies ran while one was open for 5% of the time, Pallas kernels for 0%

commit v1 on v0

--- a/solution.py
+++ b/solution.py
@@ -149,7 +149,7 @@
         precision=lax.Precision.HIGHEST,
         preferred_element_type=jnp.float32,
     )
-    gram_whole = lax.psum(gram_local, ("gx", "gy"))
+    gram_whole = lax.psum(lax.psum(gram_local, "gx"), "gy")
     orthonormal, factor = orthogonalize(tall_block, gram_whole)
     basis = (math.sqrt(rows_total) * orthonormal).reshape(sketch.shape)
     return (current, basis, factor)

time: 1210 us -> 1140 us (0.942)
  waiting for transfers between devices: 362 us -> 295 us
    psum x1 -> x2, waiting for transfers between devices: 245 us -> 178 us  [shards(): gram_whole = lax.psum(lax.psum(gram_local, 'gx'), 'gy')]
    unnamed x3 -> x4, waiting for transfers between devices: 78.1 us -> 78.1 us
  transfers between devices with their start and end apart: 34 -> 35, of which waited for: 17 -> 18; matrix products, arithmetic and copies ran while one was open for 5% -> 5% of each run, Pallas kernels for 0% -> 0%
where the time goes in v1:
time: 1140 us; the launch traced here: 1130 us
  matrix products  478 us (42%)
  waiting for transfers between devices  295 us (26%)
  loops' own time  97 us (9%)
  starting transfers between devices  89 us (8%)
  local copies, waits for them, and re-layouts  85.4 us (7%)
  other arithmetic  68.3 us (6%)
  between operations  15.6 us (1%)
    psum x2, waiting for transfers between devices, shards(): gram_whole = lax.psum(lax.psum(gram_local, 'gx'), 'gy')  178 us
    dot_general x128, matrix products, column_step(): column = jnp.dot(gram, picker, precision=lax.Precision.HIGHEST)  124 us
    dot_general x128, matrix products, column_step(): column = column - jnp.dot(lower, row_of, precision=lax.Precision.HIGHEST)  111 us
    dot_general x128, matrix products, row_step(): jnp.dot(row_of, inverse, precision=lax.Precision.HIGHEST)  107 us
    dot_general x128, matrix products, row_step(): row_of = jnp.dot(picker, lower, precision=lax.Precision.HIGHEST)  105 us
    another operation x1, loops' own time, lower_factor(): return lax.fori_loop(0, order, column_step, jnp.zeros_like(gram))  92.8 us
    unnamed x4, waiting for transfers between devices  78.1 us
    ppermute x16, starting transfers between devices, extended(): lax.ppermute(lax.slice_in_dim(block, block.shape[dim] - width, None, axis...  62.5 us
  transfers between devices with their start and end apart: 35, of which 18 were waited for; matrix products, arithmetic and copies ran while one was open for 5% of the time, Pallas kernels for 0%

profile of v1, /device:TPU:1, one launch (start us, length us, event | category | flops | bytes accessed | tf_op | source)
XLA Modules:
  0.0 1128.4 jit_solution(12860501427423339347)
XLA Ops:
  8.8 4.6 collective-permute-start
  18.1 4.4 collective-permute-done.1
  26.6 4.9 collective-permute-start.2
  35.1 3.8 fusion.119
  49.6 4.4 collective-permute-done.5
  59.1 3.6 collective-permute-start.6
  71.9 3.0 fusion.94
  76.9 3.5 collective-permute-start.8
  82.4 4.0 collective-permute-done.9
  89.0 3.7 collective-permute-start.10
  101.8 3.0 collective-permute-start.12
  107.4 4.4 collective-permute-done.13
  117.2 5.1 collective-permute-start.14
  131.9 3.4 fusion.88
  136.6 2.9 collective-permute-start.16
  141.4 6.0 slice.1072
  150.9 3.6 collective-permute-start.18
  163.3 5.1 collective-permute-start.20
  171.9 6.0 slice.1074
  185.3 3.9 collective-permute-start.22
  198.7 3.0 fusion.82
  202.2 5.1 collective-permute-start.24
  225.0 5.1 collective-permute-start.28
  233.0 4.0 collective-permute-done.29
  243.1 3.7 collective-permute-start.30
  249.5 2.8 collective-permute-done.31
  257.1 3.4 fusion.76
  266.5 78.0 %all-reduce.17.cloned.1.call-done = f32[4,48,128]{2,0,1:T(4,128)} async-done(((f32[4,48,128]{2,0,1:T(4,128)}), f32[4,48,128]{2,0,1:T(4,128)}) %all-reduce.17.cloned.1.call-update) | async-done | bytes 98320
  346.3 111.5 %all-reduce.13.cloned.1.call-done = f32[128,128]{1,0:T(8,128)} async-done(((f32[128,128]{1,0:T(8,128)}), f32[128,128]{1,0:T(8,128)}) %all-reduce.13.cloned.1.call-update) | async-done | bytes 65552 | tf_op jit(solution)/shard_map/psum | solution.py:152
  458.8 66.4 %all-reduce.15.cloned.1.call-done = f32[128,128]{1,0:T(8,128)} async-done(((f32[128,128]{1,0:T(8,128)}), f32[128,128]{1,0:T(8,128)}) %all-reduce.15.cloned.1.call-update) | async-done | bytes 65552 | tf_op jit(solution)/shard_map/psum | solution.py:152
  525.3 365.0 %while.30 = (s32[]{:T(128)}, f32[128,128]{1,0:T(8,128)S(1)}, f32[128,128]{1,0:T(8,128)}, s32[]{:T(128)}, s32[]{:T(128)}) while((s32[]{:T(128)}, f32[128,128]{1,0:T(8,128)S(1)}, f32[128,128]{1,0:T(8,128)}, s32[]{:T(128)}, s32[]{:T(128)}) %tuple.125), condition=%wide.region_8.9_spmd.clone.clone, body=%wide.region_6.8_spmd.clone.clone.sunk | while | flops 673410 | bytes 332917 | solution.py:96
  891.0 230.0 %while.29 = (s32[]{:T(128)}, f32[128,128]{1,0:T(8,128)S(1)}, f32[128,128]{1,0:T(8,128)S(1)}, s32[]{:T(128)}, s32[]{:T(128)}) while((s32[]{:T(128)}, f32[128,128]{1,0:T(8,128)S(1)}, f32[128,128]{1,0:T(8,128)S(1)}, s32[]{:T(128)}, s32[]{:T(128)}) %tuple.128), condition=%wide.region_11.12_spmd.clone, body=%wide.region_9.11_spmd.clone.sunk | while | flops 460034 | bytes 265316 | solution.py:110
  (1544 shorter events, 649.2 us)
Async XLA Ops:
  7.2 337.4 %all-reduce.17.cloned.1.call-start = ((), (), s32[]{:S(2)}) async-start(), calls=%async_computation.2 | async-start | bytes 196608
  8.8 9.3 collective-permute-start
  13.4 9.1 collective-permute-start.1
  25.3 16.2 %collective-permute-start.3 = (f32[3,32,12,2]{1,3,2,0:T(2,128)}, f32[3,32,12,2]{1,3,2,0:T(2,128)}, u32[]{:S(2)}, u32[]{:S(2)}) collective-permute-start(f32[3,32,12,2]{1,3,2,0:T(2,128)} %get-tuple-element.276), channel_id=1, source_target_pairs={{1,0},{2,1},{3,2},{4,3},{5,4},{6,5},{7,6},{9,8},{10,9},{11,10},{12... | collective-permute-start | bytes 27656 | tf_op jit(solution)/shard_map/ppermute | solution.py:19
  26.6 13.8 %collective-permute-start.2 = (f32[3,32,12,2]{1,3,2,0:T(2,128)}, f32[3,32,12,2]{1,3,2,0:T(2,128)}, u32[]{:S(2)}, u32[]{:S(2)}) collective-permute-start(f32[3,32,12,2]{1,3,2,0:T(2,128)} %get-tuple-element.277), channel_id=1, source_target_pairs={{0,1},{1,2},{2,3},{3,4},{4,5},{5,6},{6,7},{8,9},{9,10},{10,11},{11... | collective-permute-start | bytes 27656 | tf_op jit(solution)/shard_map/ppermute | solution.py:16
  47.0 7.0 collective-permute-start.5
  59.1 10.4 collective-permute-start.6
  62.7 5.4 collective-permute-start.7
  76.9 5.5 collective-permute-start.8
  80.4 5.9 collective-permute-start.9
  89.0 9.1 collective-permute-start.10
  92.8 5.1 collective-permute-start.11
  101.8 5.6 collective-permute-start.12
  104.8 7.0 collective-permute-start.13
  117.2 13.2 %collective-permute-start.14 = (f32[6,32,12,2]{1,3,2,0:T(2,128)S(1)}, f32[6,32,12,2]{1,3,2,0:T(2,128)S(1)}, u32[]{:S(2)}, u32[]{:S(2)}) collective-permute-start(f32[6,32,12,2]{1,3,2,0:T(2,128)S(1)} %copy.329), channel_id=1, source_target_pairs={{0,1},{1,2},{2,3},{3,4},{4,5},{5,6},{6,7},{8,9},{9,10},{10,11},{11... | collective-permute-start | bytes 55304 | tf_op jit(solution)/shard_map/ppermute | solution.py:16
  122.3 5.7 collective-permute-start.15
  136.6 11.5 %collective-permute-start.16 = (f32[3,32,2,128]{3,1,2,0:T(8,128)S(1)}, f32[3,32,2,128]{3,1,2,0:T(8,128)S(1)}, u32[]{:S(2)}, u32[]{:S(2)}) collective-permute-start(f32[3,32,2,128]{3,1,2,0:T(8,128)S(1)} %get-tuple-element.316), channel_id=1, source_target_pairs={{0,8},{8,16},{16,24},{24,32},{32,40},{40,48},{48,56},{56,64},{64,7... | collective-permute-start | bytes 294920 | tf_op jit(solution)/shard_map/ppermute | solution.py:16
  139.5 8.6 collective-permute-start.17
  150.9 8.8 collective-permute-start.18
  163.3 15.3 %collective-permute-start.20 = (f32[6,32,2,128]{3,1,2,0:T(8,128)S(1)}, f32[6,32,2,128]{3,1,2,0:T(8,128)S(1)}, u32[]{:S(2)}, u32[]{:S(2)}) collective-permute-start(f32[6,32,2,128]{3,1,2,0:T(8,128)S(1)} %get-tuple-element.294), channel_id=1, source_target_pairs={{0,8},{8,16},{16,24},{24,32},{32,40},{40,48},{48,56},{56,64},{64,7... | collective-permute-start | bytes 589832 | tf_op jit(solution)/shard_map/ppermute | solution.py:16
  168.4 10.2 collective-permute-start.21
  185.3 11.0 collective-permute-start.22
  189.3 5.7 collective-permute-start.23
  202.2 11.8 %collective-permute-start.24 = (f32[3,32,2,128]{3,1,2,0:T(8,128)S(1)}, f32[3,32,2,128]{3,1,2,0:T(8,128)S(1)}, u32[]{:S(2)}, u32[]{:S(2)}) collective-permute-start(f32[3,32,2,128]{3,1,2,0:T(8,128)S(1)} %get-tuple-element.312), channel_id=1, source_target_pairs={{0,8},{8,16},{16,24},{24,32},{32,40},{40,48},{48,56},{56,64},{64,7... | collective-permute-start | bytes 294920 | tf_op jit(solution)/shard_map/ppermute | solution.py:16
  207.3 6.7 collective-permute-start.25
  214.9 7.5 collective-permute-start.26
  225.0 8.0 collective-permute-start.28
  230.1 7.0 collective-permute-start.29
  243.1 11.6 %collective-permute-start.30 = (f32[6,32,12,2]{1,3,2,0:T(2,128)S(1)}, f32[6,32,12,2]{1,3,2,0:T(2,128)}, u32[]{:S(2)}, u32[]{:S(2)}) collective-permute-start(f32[6,32,12,2]{1,3,2,0:T(2,128)S(1)} %copy.351), channel_id=1, source_target_pairs={{0,1},{1,2},{2,3},{3,4},{4,5},{5,6},{6,7},{8,9},{9,10},{10,11},{11... | collective-permute-start | bytes 55304 | tf_op jit(solution)/shard_map/ppermute | solution.py:16
  246.9 5.4 collective-permute-start.31
  265.2 192.6 %all-reduce.13.cloned.1.call-start = ((), (), s32[]{:S(2)}) async-start(), calls=%async_computation | async-start | bytes 131072 | tf_op jit(solution)/shard_map/psum | solution.py:152
  346.2 179.0 %all-reduce.15.cloned.1.call-start = ((), (), s32[]{:S(2)}) async-start(), calls=%async_computation.1 | async-start | bytes 131072 | tf_op jit(solution)/shard_map/psum | solution.py:152
  (45 other events, 216.0 us)
Sparse Core Ops, SparseCore 0:
  265.3 79.1 all-reduce.16
  348.7 109.0 all-reduce.12
  460.1 65.1 all-reduce.14
